TPU v7x, 32 devices: a whole 2x2x4 slice. The times are simulated.
32 devices in a mesh: slab: 16 (over z, y, x), pencil: 2 (over core).
Axes of the slice: x: 2, y: 2, z: 4, core: 2. Of those that a mesh axis runs over, the one named last changes fastest.
Arguments:
- owner_map: int32 [16], replicated, may hold values from 0 to 15
- window_start: int32 [1], replicated, may hold values from 0 to 8
- child_maps: float32 [8, 20, 20], replicated, may hold values from -1 to 1
- innovation: float32 [20, 20], replicated, may hold values from -1.25 to 1.25
- coarse_bank: float32 [16, 20, 74898], P('slab'), may hold values from -6 to 6
- noise_middle: float32 [20, 64, 64, 128], P(None, 'slab', 'pencil'), may hold values from -6 to 6
- noise_finest: float32 [20, 128, 128, 256], P(None, 'slab', 'pencil'), may hold values from -6 to 6
Outputs:
- field_values: float32 [256, 256, 512], P('slab', 'pencil')
- zface_mean: float32 [128, 256, 512], P('slab', 'pencil')
- yface_mean: float32 [256, 128, 512], P('slab', 'pencil')
All inputs are finite; a program needn't handle non-finite values.
Results may differ from a plain program's by a relative error of at most 0.0001.
Values sent between devices are 32-bit elements; how exact they have to be, the bound alone decides.
A program may use at most 448 MiB of HBM per device.

v0:
```python
import math
import jax
import jax.numpy as jnp
import numpy as np
from jax import lax
from jax.sharding import PartitionSpec as P

LEVELS = 8
ROOTS = 2
ROOTS_Z = 1
ROOTS_Y = 1


def from_root(block, axis, owner):
    block = jnp.where(lax.axis_index(axis) == owner, block, jnp.zeros_like(block))
    return lax.psum(block, axis)


def shifted(block, axis, distance):
    devices = range(lax.axis_size(axis))
    route = [((i - distance) % len(devices), i) for i in devices]
    return lax.ppermute(block, axis, route)


def legendre(order, point):
    values = [1.0, point, 1.5 * point * point - 0.5, 2.5 * point * point * point - 1.5 * point]
    return values[order]


def basis_table(points):
    table_rows = []
    for point in points:
        w_coord, v_coord, u_coord = point
        entry = []
        for deg_x in range(4):
            for deg_y in range(4):
                for deg_z in range(4):
                    if deg_x + deg_y + deg_z <= 3:
                        factor = math.sqrt((2 * deg_x + 1) * (2 * deg_y + 1) * (2 * deg_z + 1))
                        entry.append(
                            factor
                            * legendre(deg_x, u_coord)
                            * legendre(deg_y, v_coord)
                            * legendre(deg_z, w_coord)
                        )
        table_rows.append(entry)
    return jnp.asarray(np.array(table_rows), jnp.float32)


def level_span(level):
    first = ROOTS_Z * ROOTS_Y * ROOTS
    return (first * (8**level - 1) // 7, first * 8**level)


def level_block(flat, level):
    scale = 2**level
    offset, length = level_span(level)
    return flat[:, offset : offset + length].reshape(
        flat.shape[0], ROOTS_Z * scale, ROOTS_Y * scale, ROOTS * scale
    )


def descend(parent, child_maps):
    kids = jnp.einsum("okn,nzyx->okzyx", child_maps, parent, precision=lax.Precision.HIGHEST)
    count, planes, rows_y, cols_x = parent.shape
    kids = kids.reshape(2, 2, 2, count, planes, rows_y, cols_x).transpose(3, 4, 0, 5, 1, 6, 2)
    return kids.reshape(count, 2 * planes, 2 * rows_y, 2 * cols_x)


def innovate(innovation, noise):
    return jnp.einsum("kn,nzyx->kzyx", innovation, noise, precision=lax.Precision.HIGHEST)


def expand(table, coeffs):
    return jnp.einsum("pk,kzyx->pzyx", table, coeffs, precision=lax.Precision.HIGHEST)


def refine(coeffs, child_maps, plane_start, planes, row_start, rows):
    zero = jnp.zeros((), jnp.int32)
    plane_start = jnp.asarray(plane_start, jnp.int32)
    row_start = jnp.asarray(row_start, jnp.int32)
    parent_start = plane_start // 2
    parent_row = row_start // 2
    parent_planes = max(1, planes // 2)
    parent_rows = max(1, rows // 2)
    count = coeffs.shape[0]
    parents = lax.dynamic_slice(
        coeffs,
        (zero, parent_start, parent_row, zero),
        (count, parent_planes, parent_rows, coeffs.shape[3]),
    )
    spread = descend(parents, child_maps)
    return lax.dynamic_slice(
        spread,
        (zero, plane_start - 2 * parent_start, row_start - 2 * parent_row, zero),
        (count, planes, rows, spread.shape[3]),
    )


def shards(
    owner_map, window_start, child_maps, innovation, coarse_bank, noise_middle, noise_finest
):
    bank_levels = LEVELS - 2
    last_level = bank_levels - 1
    local_bank = coarse_bank[0]
    owners = [owner_map[window_start[0] + level] for level in range(bank_levels)]
    position = lax.axis_index("slab")
    coeffs = None
    received = [
        from_root(level_block(local_bank, level), "slab", owners[level])
        for level in range(last_level)
    ]
    for level in range(last_level):
        fresh = innovate(innovation, received[level])
        coeffs = fresh if level == 0 else descend(coeffs, child_maps) + fresh
    count, planes, rows_y, cols_x = noise_middle.shape
    first_plane = position * planes
    first_row = lax.axis_index("pencil") * rows_y
    top_start = first_plane // 2
    top_row = first_row // 2
    top_planes = max(1, planes // 2)
    top_rows = max(1, rows_y // 2)
    scale = 2**last_level
    bank_cols = ROOTS * scale
    zero = jnp.zeros((), jnp.int32)
    whole_bank = from_root(level_block(local_bank, last_level), "slab", owners[last_level])
    noise_top = lax.dynamic_slice(
        whole_bank, (zero, top_start, top_row, zero), (count, top_planes, top_rows, bank_cols)
    )
    upper_level = refine(coeffs, child_maps, top_start, top_planes, top_row, top_rows) + innovate(
        innovation, noise_top
    )
    middle = refine(
        upper_level,
        child_maps,
        first_plane - 2 * top_start,
        planes,
        first_row - 2 * top_row,
        rows_y,
    ) + innovate(innovation, noise_middle)
    fine = descend(middle, child_maps) + innovate(innovation, noise_finest)
    count, fine_planes, fine_rows, fine_cols = fine.shape
    halves = [-0.5, 0.5]
    inner = basis_table([(pz, py, px) for pz in halves for py in halves for px in halves])
    top = basis_table([(1.0, py, px) for py in halves for px in halves])
    bottom = basis_table([(-1.0, py, px) for py in halves for px in halves])
    north = basis_table([(pz, 1.0, px) for pz in halves for px in halves])
    south = basis_table([(pz, -1.0, px) for pz in halves for px in halves])
    values = (
        expand(inner, fine)
        .reshape(2, 2, 2, fine_planes, fine_rows, fine_cols)
        .transpose(3, 0, 4, 1, 5, 2)
    )
    field_values = values.reshape(2 * fine_planes, 2 * fine_rows, 2 * fine_cols)
    lower_faces = expand(bottom, fine)
    south_faces = expand(south, fine)
    above_coeffs = shifted(fine[:, :1], "slab", -1)
    beside_coeffs = shifted(fine[:, :, :1], "pencil", -1)
    above = expand(bottom, above_coeffs)
    beside = expand(south, beside_coeffs)
    lower_next = jnp.concatenate([lower_faces[:, 1:], above], axis=1)
    south_next = jnp.concatenate([south_faces[:, :, 1:], beside], axis=2)
    zsum = expand(top, fine) + lower_next
    zface = (0.5 * zsum).reshape(2, 2, fine_planes, fine_rows, fine_cols).transpose(2, 3, 0, 4, 1)
    zface_mean = zface.reshape(fine_planes, 2 * fine_rows, 2 * fine_cols)
    ysum = expand(north, fine) + south_next
    yface = (0.5 * ysum).reshape(2, 2, fine_planes, fine_rows, fine_cols).transpose(2, 0, 3, 4, 1)
    yface_mean = yface.reshape(2 * fine_planes, fine_rows, 2 * fine_cols)
    return (field_values, zface_mean, yface_mean)


def solution(mesh):
    placed = (
        P(),
        P(),
        P(),
        P(),
        P("slab", None, None),
        P(None, "slab", "pencil", None),
        P(None, "slab", "pencil", None),
    )
    return jax.shard_map(
        shards,
        mesh=mesh,
        in_specs=placed,
        out_specs=(P("slab", "pencil", None), P("slab", "pencil", None), P("slab", "pencil", None)),
        check_vma=False,
    )
```

profile of v0, /device:TPU:0, one launch (start us, length us, event | category | flops | bytes accessed | tf_op | source)
XLA Modules:
  0.0 1258.6 jit_solution(5010336957763130200)
XLA Ops:
  8.0 1.5 fusion.49
  11.5 26.7 %copy.91 = f32[1,20,74898]{1,2,0:T(8,128)} copy(f32[1,20,74898]{2,0,1:T(1,128)} %param.16) | data formatting | bytes 11983680 | tf_op args[4]
  38.2 1.9 slice_select_fusion.2
  40.1 4.6 slice_select_fusion.1
  44.7 22.8 %slice_select_fusion = f32[20,65536]{0,1:T(8,128)} fusion(f32[20,74898]{0,1:T(8,128)} %bitcast.227, pred[]{:T(512)S(6)} %eq.23), kind=kLoop, calls=%fused_computation | loop fusion | flops 1310720 | bytes 10485761 | tf_op jit(solution)/shard_map/jit(_where)/select_n | solution.py:15
  67.5 23.8 %copy.108 = f32[20,32,32,64]{3,0,2,1:T(8,128)} copy(f32[20,32,32,64]{0,3,2,1:T(8,128)} %bitcast.231) | data formatting | bytes 10485760 | tf_op jit(solution)/shard_map/jit(_where)/select_n | solution.py:15
  91.3 5.5 copy.103
  98.6 0.7 slice_select_fusion.5
  99.3 0.7 slice_select_fusion.4
  100.0 0.9 slice_select_fusion.3
  100.9 85.6 %all-reduce = (f32[20,2]{0,1:T(2,128)S(1)}, f32[20,2,2,4]{0,3,2,1:T(4,128)S(1)}, f32[20,4,4,8]{0,3,2,1:T(8,128)S(1)}) all-reduce(f32[20,2]{0,1:T(2,128)S(1)} %slice_select_fusion.5, f32[20,2,2,4]{0,3,2,1:T(4,128)S(1)} %bitcast.254, f32[20,4,4,8]{0,3,2,1:T(8,128)S(1)} %bitcast.252), channel_id=1, replica_groups=mesh['slab'=16,'pencil'=2] {'slab'}, use_global_device_ids=true, to_apply=%region_0.1 | all-reduce | flops 2920 | bytes 23360 | tf_op jit(solution)/shard_map/psum | solution.py:16
  186.7 0.6 convolution_bitcast_fusion.6
  187.5 0.6 fusion.35
  188.4 0.7 fusion.33
  189.3 3.2 fusion.12
  192.5 348.9 %all-reduce.4.cloned.1.call-done = (f32[20,8,8,16]{0,3,2,1:T(8,128)}, f32[20,16,16,32]{3,0,2,1:T(8,128)}, f32[20,32,32,64]{3,0,2,1:T(8,128)}) async-done(((f32[20,8,8,16]{0,3,2,1:T(8,128)}, f32[20,16,16,32]{3,0,2,1:T(8,128)}, f32[20,32,32,64]{3,0,2,1:T(8,128)}), (f32[20,8,8,16]{0,3,2,1:T(8,128)}, f32[20,16,16,32]{3,0,2,1:T(8,128)}, f32[20,32,32,64]{3,0,2,1:T(8,128)})) %all-reduce.4.cloned.1.call-update) | async-done | bytes 5980176 | tf_op jit(solution)/shard_map/psum | solution.py:16
  541.4 6.4 convolution_bitcast_fusion
  548.4 3.5 fusion.31
  551.9 2.9 copy.101
  554.9 1.7 convolution_bitcast_fusion.1
  556.6 0.7 copy.106
  557.7 1.5 fusion.18
  559.1 4.3 fusion.29
  563.4 12.3 copy.111
  575.7 5.2 copy.113
  581.0 13.9 %fusion.7 = f32[4,32,128,8,20]{2,4,3,1,0:T(8,128)} fusion(f32[20,4,32,128]{3,0,2,1:T(8,128)S(1)} %copy.113, f32[20,4,32,128]{3,0,2,1:T(8,128)} %fusion.12, f32[8,20,20,1,1]{2,0,1,4,3:T(8,128)S(1)} %bitcast.245), kind=kOutput, calls=%fused_computation.10 | convolution fusion | flops 629473280 | bytes 13120000 | tf_op jit(solution)/shard_map/okn,nzyx->okzyx/dot_general | solution.py:64
  594.8 78.5 %copy.115 = f32[2,2,2,20,4,32,128]{3,2,6,1,5,0,4:T(2,128)} copy(f32[2,2,2,20,4,32,128]{6,3,2,1,0,5,4:T(8,128)} %bitcast.233) | data formatting | bytes 20971520 | tf_op jit(solution)/shard_map/reshape | solution.py:66
  673.4 38.4 %copy.117 = f32[20,8,64,256]{3,0,2,1:T(8,128)} copy(f32[20,8,64,256]{0,3,2,1:T(8,128)} %bitcast.73) | data formatting | bytes 20971520 | tf_op jit(solution)/shard_map/reshape | solution.py:67
  711.8 23.1 %fusion.2 = f32[20,8,64,256]{3,0,2,1:T(8,128)S(1)} fusion(f32[20,8,64,256]{3,0,2,1:T(8,128)} %copy.117, f32[20,8,64,256]{3,2,1,0:T(8,128)} %param.18, f32[20,20]{1,0:T(8,128)S(1)} %copy-done.5), kind=kOutput, calls=%fused_computation.3 | convolution fusion | flops 631767040 | bytes 31458880 | tf_op jit(solution)/shard_map/kn,nzyx->kzyx/dot_general | solution.py:71
  735.0 0.7 slice.47
  735.9 1.5 copy.119
  737.3 3.2 collective-permute-start
  740.6 7.7 fusion.50
  748.3 86.5 %fusion.52 = f32[4,8,63,256]{3,0,2,1:T(4,128)} fusion(f32[4,20,1,1]{1,0,3,2:T(4,128)S(1)} %copy-done.12, f32[20,8,64,256]{3,0,2,1:T(8,128)S(1)} %fusion.2), kind=kOutput, calls=%fused_computation.67 | convolution fusion | flops 123863040 | bytes 12550464 | tf_op jit(solution)/shard_map/slice | solution.py:162
  834.8 16.2 %fusion.51 = f32[4,7,64,256]{3,0,2,1:T(4,128)} fusion(f32[4,20,1,1]{1,0,3,2:T(4,128)S(1)} %copy-done.7, f32[20,8,64,256]{3,0,2,1:T(8,128)S(1)} %fusion.2), kind=kOutput, calls=%fused_computation.66 | convolution fusion | flops 110100480 | bytes 12321088 | tf_op jit(solution)/shard_map/slice | solution.py:161
  850.9 5.8 reshape.129
  856.8 119.4 %copy.118 = f32[2,2,2,8,64,256]{2,5,1,4,0,3:T(8,128)} copy(f32[2,2,2,8,64,256]{5,2,1,0,4,3:T(2,128)} %reshape.129) | data formatting | bytes 8388608 | tf_op jit(solution)/shard_map/reshape | solution.py:151
  976.2 183.6 %reshape.130 = f32[16,128,512]{2,1,0:T(8,128)} reshape(f32[8,2,64,2,256,2]{5,4,3,2,1,0:T(8,128)} %bitcast.74) | data formatting | bytes 8388608 | tf_op jit(solution)/shard_map/reshape | solution.py:154
  1159.9 1.1 convolution_bitcast_fusion.5
  1161.0 10.3 fusion.6
  1171.3 2.9 reshape.135
  1174.3 4.4 copy.122
  1178.6 3.9 copy.124
  1182.6 2.9 fusion.19
  1185.5 9.6 fusion.5
  1195.1 2.6 reshape.132
  1197.7 33.7 %copy.121 = f32[2,2,8,64,256]{2,1,4,0,3:T(2,128)} copy(f32[2,2,8,64,256]{4,1,0,3,2:T(2,128)} %reshape.132) | data formatting | bytes 4194304 | tf_op jit(solution)/shard_map/reshape | solution.py:164
  1231.4 20.2 %copy.123 = f32[8,128,512]{2,1,0:T(8,128)} copy(f32[8,128,512]{0,2,1:T(8,128)} %bitcast.232) | data formatting | bytes 4194304
  (44 shorter events, 2.2 us)
Async XLA Ops:
  7.2 182.2 %copy-start = (f32[20,4,32,128]{3,2,1,0:T(8,128)S(1)}, f32[20,4,32,128]{3,2,1,0:T(8,128)}, u32[]{:S(2)}) copy-start(f32[20,4,32,128]{3,2,1,0:T(8,128)} %param.17) | copy-start | bytes 3932164
  7.2 534.3 %all-reduce.4.cloned.1.call-start = ((), (), s32[]{:S(2)}) async-start(), calls=%async_computation | async-start | bytes 32505856 | tf_op jit(solution)/shard_map/psum | solution.py:16
  96.8 89.8 %copy-start.5 = (f32[20,20]{1,0:T(8,128)S(1)}, f32[20,20]{1,0:T(8,128)}, u32[]{:S(2)}) copy-start(f32[20,20]{1,0:T(8,128)} %param.15) | copy-start | bytes 4804
  96.8 90.0 %copy-start.4 = (f32[8,20,20]{2,0,1:T(8,128)S(1)}, f32[8,20,20]{2,0,1:T(8,128)}, u32[]{:S(2)}) copy-start(f32[8,20,20]{2,0,1:T(8,128)} %param.14) | copy-start | bytes 38404
  541.4 6.4 copy-start.6
  734.9 99.8 %copy-start.2 = (f32[20,8,64,256]{3,0,2,1:T(8,128)}, f32[20,8,64,256]{3,0,2,1:T(8,128)S(1)}, u32[]{:S(2)}) copy-start(f32[20,8,64,256]{3,0,2,1:T(8,128)S(1)} %fusion.2) | copy-start | bytes 31457284
  735.0 5.6 copy-start.8
  735.8 424.1 %collective-permute-start.1 = (f32[20,8,1,256]{3,0,2,1:T(8,128)}, f32[20,8,1,256]{3,0,2,1:T(8,128)}, u32[]{:S(2)}, u32[]{:S(2)}) collective-permute-start(f32[20,8,1,256]{3,0,2,1:T(8,128)} %slice.47), channel_id=1, source_target_pairs={{1,0},{0,1},{3,2},{2,3},{5,4},{4,5},{7,6},{6,7},{9,8},{8,9},{11,10... | collective-permute-start | bytes 491528 | tf_op jit(solution)/shard_map/ppermute | solution.py:22
  737.3 11.0 copy-start.12
  737.3 445.2 %collective-permute-start = (f32[20,1,64,256]{3,2,1,0:T(8,128)}, f32[20,1,64,256]{3,2,1,0:T(8,128)}, u32[]{:S(2)}, u32[]{:S(2)}) collective-permute-start(f32[20,1,64,256]{3,2,1,0:T(8,128)} %copy.119), channel_id=1, source_target_pairs={{2,0},{4,2},{6,4},{8,6},{10,8},{12,10},{14,12},{16,14},{18,16},{20... | collective-permute-start | bytes 3932168 | tf_op jit(solution)/shard_map/ppermute | solution.py:22
  748.3 86.5 %copy-start.7 = (f32[4,20,1,1]{1,0,3,2:T(4,128)S(1)}, f32[4,20,1,1]{1,0,3,2:T(4,128)}, u32[]{:S(2)}) copy-start(f32[4,20,1,1]{1,0,3,2:T(4,128)} %constant.107) | copy-start | bytes 964
  976.2 183.6 %copy-start.11 = (f32[4,20,1]{1,0,2:T(4,128)S(1)}, f32[4,20,1]{1,0,2:T(4,128)}, u32[]{:S(2)}) copy-start(f32[4,20,1]{1,0,2:T(4,128)} %constant.111) | copy-start | bytes 964
  976.2 184.8 %copy-start.3 = (f32[4,8,63,256]{3,0,2,1:T(4,128)S(1)}, f32[4,8,63,256]{3,0,2,1:T(4,128)}, u32[]{:S(2)}) copy-start(f32[4,8,63,256]{3,0,2,1:T(4,128)} %fusion.52) | copy-start | bytes 6193156
  976.2 184.8 %copy-start.10 = (f32[4,20,1,1]{1,0,3,2:T(4,128)S(1)}, f32[4,20,1,1]{1,0,3,2:T(4,128)}, u32[]{:S(2)}) copy-start(f32[4,20,1,1]{1,0,3,2:T(4,128)} %constant.109) | copy-start | bytes 964
  1178.6 3.9 copy-start.13
  1178.6 6.9 copy-start.9
  1231.4 20.2 %copy-start.1 = (f32[20,4,32,128]{3,2,1,0:T(8,128)S(1)}, f32[20,4,32,128]{3,2,1,0:T(8,128)}, u32[]{:S(2)}) copy-start(f32[20,4,32,128]{3,2,1,0:T(8,128)} %param.17) | copy-start | bytes 3932164
Sparse Core Ops, SparseCore 0:
  96.9 444.4 all-reduce.3
where the time goes:
time: 1280 us; the launch traced here: 1260 us
  local copies, waits for them, and re-layouts  575 us (45%)
  waiting for transfers between devices  349 us (27%)
  matrix products  195 us (15%)
  blocking collectives  85.6 us (7%)
  other arithmetic  31.6 us (2%)
  between operations  19.1 us (1%)
    psum x1, waiting for transfers between devices, from_root(): return lax.psum(block, axis)  349 us
    reshape x1, local copies, waits for them, and re-layouts, shards(): field_values = values.reshape(2 * fine_planes, 2 * fine_rows, 2 * fine_cols)  184 us
    reshape x2, local copies, waits for them, and re-layouts, shards(): values = expand(inner, fine).reshape(2, 2, 2, fine_planes, fine_rows, fin...  125 us
    reshape x3, local copies, waits for them, and re-layouts, descend(): kids.reshape(2, 2, 2, count, planes, rows_y, cols_x)  93.8 us
    slice x1, matrix products, shards(): south_next = jnp.concatenate([south_faces[:, :, 1:], beside], axis=2)  86.5 us
    psum x1, blocking collectives, from_root(): return lax.psum(block, axis)  85.6 us
    unnamed x32, local copies, waits for them, and re-layouts  51 us
    reshape x3, local copies, waits for them, and re-layouts, descend(): return kids.reshape(count, 2 * planes, 2 * rows_y, 2 * cols_x)  44.1 us
  transfers between devices with their start and end apart: 3, of which 1 were waited for; matrix products, arithmetic and copies ran while one was open for 36% of the time, Pallas kernels for 0%

commit v1 on v0

--- a/solution.py
+++ b/solution.py
@@ -13,7 +13,7 @@
 
 def from_root(block, axis, owner):
     block = jnp.where(lax.axis_index(axis) == owner, block, jnp.zeros_like(block))
-    return lax.psum(block, axis)
+    return jnp.sum(lax.all_gather(block, axis), axis=0)
 
 
 def shifted(block, axis, distance):

time: 1280 us -> 2990 us (2.34)
  waiting for transfers between devices: 349 us -> 1930 us
  other arithmetic: 31.6 us -> 115 us
  blocking collectives: 85.6 us -> 138 us
    all_gather x0 -> x3, waiting for transfers between devices: none -> 1930 us  [from_root(): return jnp.sum(lax.all_gather(block, axis), axis=0)]
    psum x1 -> x0, waiting for transfers between devices: 349 us -> none  [from_root(): return lax.psum(block, axis)]
    all_gather x0 -> x3, blocking collectives: none -> 138 us  [from_root(): return jnp.sum(lax.all_gather(block, axis), axis=0)]
    psum x1 -> x0, blocking collectives: 85.6 us -> none  [from_root(): return lax.psum(block, axis)]
    reduce_sum x0 -> x6, other arithmetic: none -> 83 us  [from_root(): return jnp.sum(lax.all_gather(block, axis), axis=0)]
  transfers between devices with their start and end apart: 3 -> 5, of which waited for: 1 -> 2; matrix products, arithmetic and copies ran while one was open for 36% -> 19% of each run, Pallas kernels for 0% -> 0%
where the time goes in v1:
time: 2990 us; the launch traced here: 2970 us
  waiting for transfers between devices  1930 us (65%)
  local copies, waits for them, and re-layouts  575 us (19%)
  matrix products  194 us (6%)
  blocking collectives  138 us (5%)
  other arithmetic  115 us (4%)
    all_gather x3, waiting for transfers between devices, from_root(): return jnp.sum(lax.all_gather(block, axis), axis=0)  1930 us
    reshape x1, local copies, waits for them, and re-layouts, shards(): field_values = values.reshape(2 * fine_planes, 2 * fine_rows, 2 * fine_cols)  184 us
    all_gather x3, blocking collectives, from_root(): return jnp.sum(lax.all_gather(block, axis), axis=0)  138 us
    reshape x2, local copies, waits for them, and re-layouts, shards(): values = expand(inner, fine).reshape(2, 2, 2, fine_planes, fine_rows, fin...  125 us
    reshape x3, local copies, waits for them, and re-layouts, descend(): kids.reshape(2, 2, 2, count, planes, rows_y, cols_x)  93.1 us
    slice x1, matrix products, shards(): south_next = jnp.concatenate([south_faces[:, :, 1:], beside], axis=2)  86.5 us
    reduce_sum x6, other arithmetic, from_root(): return jnp.sum(lax.all_gather(block, axis), axis=0)  83 us
  transfers between devices with their start and end apart: 5, of which 2 were waited for; matrix products, arithmetic and copies ran while one was open for 19% of the time, Pallas kernels for 0%

profile of v1, /device:TPU:0, one launch (start us, length us, event | category | flops | bytes accessed | tf_op | source)
XLA Modules:
  0.0 2970.2 jit_solution(15621516815495878565)
XLA Ops:
  8.0 26.8 copy.58
  36.1 1.9 slice_select_fusion.2
  38.7 4.6 slice_select_fusion.1
  43.3 5.4 copy.69
  49.4 23.0 slice_select_fusion
  72.4 23.7 copy.75
  98.7 44.2 %all-gather.1 = f32[16,20,2]{1,2,0:T(2,128)S(1)} all-gather(f32[1,20,2]{1,2,0:T(2,128)S(1)} %fusion.52), channel_id=2, replica_groups=mesh['slab'=16,'pencil'=2] {'slab'}, dimensions={0}, use_global_device_ids=true | all-gather | bytes 2720 | tf_op jit(solution)/shard_map/all_gather | solution.py:16
  143.7 0.7 slice_select_fusion.4
  144.4 37.5 %all_gather.28 = f32[16,20,2,2,4]{1,4,3,2,0:T(4,128)S(1)} all-gather(f32[1,20,2,2,4]{1,4,3,2,0:T(4,128)S(1)} %bitcast.255), channel_id=1, replica_groups=mesh['slab'=16,'pencil'=2] {'slab'}, dimensions={0}, use_global_device_ids=true | all-gather | bytes 21760 | tf_op jit(solution)/shard_map/all_gather | solution.py:16
  182.7 0.9 slice_select_fusion.3
  183.6 56.9 %all_gather.29 = f32[16,20,4,4,8]{1,4,3,2,0:T(8,128)S(1)} all-gather(f32[1,20,4,4,8]{1,4,3,2,0:T(8,128)S(1)} %bitcast.253), channel_id=1, replica_groups=mesh['slab'=16,'pencil'=2] {'slab'}, dimensions={0}, use_global_device_ids=true | all-gather | bytes 174080 | tf_op jit(solution)/shard_map/all_gather | solution.py:16
  241.8 3.2 fusion.17
  245.0 4.8 reduce_sum.57
  250.3 3.5 fusion.36
  253.8 2.4 copy.68
  256.3 339.2 %all-gather.8.cloned.1.call-done = f32[16,20,16,16,32]{4,3,2,1,0:T(8,128)} async-done(((f32[1,20,16,16,32]{4,3,2,1,0:T(8,128)}), f32[16,20,16,16,32]{4,3,2,1,0:T(8,128)}) %all-gather.8.cloned.1.call-update) | async-done | bytes 10485776 | tf_op jit(solution)/shard_map/all_gather | solution.py:16
  595.6 22.8 reduce_sum.58
  618.4 7.0 fusion.9
  625.4 0.8 convolution_bitcast_fusion
  627.3 1587.9 %all-gather.10.cloned.1.call-done = f32[16,20,32,32,64]{4,3,2,1,0:T(8,128)} async-done(((f32[1,20,32,32,64]{4,3,2,1,0:T(8,128)}), f32[16,20,32,32,64]{4,3,2,1,0:T(8,128)}) %all-gather.10.cloned.1.call-update) | async-done | bytes 83886096 | tf_op jit(solution)/shard_map/all_gather | solution.py:16
  2215.2 55.3 %reduce_sum.59 = f32[20,32,32,64]{3,2,1,0:T(8,128)} reduce(f32[16,20,32,32,64]{4,3,2,1,0:T(8,128)} %all-gather.10.cloned.1.call-done, f32[]{:T(128)} %constant.84.clone.1), dimensions={0}, to_apply=%region_5.6 | reduce | flops 19660800 | bytes 89128960 | tf_op jit(solution)/shard_map/reduce_sum | solution.py:16
  2270.4 1.1 constant_dynamic-slice_fusion.1
  2272.2 4.3 fusion.34
  2276.5 12.3 copy.80
  2288.8 5.2 copy.82
  2294.0 14.0 fusion.12
  2308.0 78.4 %copy.84 = f32[2,2,2,20,4,32,128]{3,2,6,1,5,0,4:T(2,128)} copy(f32[2,2,2,20,4,32,128]{6,3,2,1,0,5,4:T(8,128)} %bitcast.234) | data formatting | bytes 20971520 | tf_op jit(solution)/shard_map/reshape | solution.py:66
  2386.4 38.4 %copy.86 = f32[20,8,64,256]{3,0,2,1:T(8,128)} copy(f32[20,8,64,256]{0,3,2,1:T(8,128)} %bitcast.74) | data formatting | bytes 20971520 | tf_op jit(solution)/shard_map/reshape | solution.py:67
  2424.9 23.0 fusion.2
  2447.9 0.7 slice.47
  2448.8 1.5 copy.88
  2450.2 2.3 collective-permute-start
  2452.5 7.7 fusion.55
  2460.3 86.5 %fusion.57 = f32[4,8,63,256]{3,0,2,1:T(4,128)} fusion(f32[4,20,1,1]{1,0,3,2:T(4,128)S(1)} %copy-done.12, f32[20,8,64,256]{3,0,2,1:T(8,128)S(1)} %fusion.2), kind=kOutput, calls=%fused_computation.70 | convolution fusion | flops 123863040 | bytes 12550464 | tf_op jit(solution)/shard_map/slice | solution.py:162
  2546.7 16.2 fusion.56
  2562.9 5.8 reshape.179
  2568.7 119.3 %copy.87 = f32[2,2,2,8,64,256]{2,5,1,4,0,3:T(8,128)} copy(f32[2,2,2,8,64,256]{5,2,1,0,4,3:T(2,128)} %reshape.179) | data formatting | bytes 8388608 | tf_op jit(solution)/shard_map/reshape | solution.py:151
  2688.0 183.6 %reshape.180 = f32[16,128,512]{2,1,0:T(8,128)} reshape(f32[8,2,64,2,256,2]{5,4,3,2,1,0:T(8,128)} %bitcast.75) | data formatting | bytes 8388608 | tf_op jit(solution)/shard_map/reshape | solution.py:154
  2871.7 1.1 convolution_bitcast_fusion.4
  2872.8 10.3 fusion.8
  2883.1 2.9 reshape.185
  2886.1 4.4 copy.91
  2890.4 3.9 copy.93
  2894.4 2.9 fusion.24
  2897.3 9.6 fusion.7
  2906.9 2.6 reshape.182
  2909.5 33.8 %copy.90 = f32[2,2,8,64,256]{2,1,4,0,3:T(2,128)} copy(f32[2,2,8,64,256]{4,1,0,3,2:T(2,128)} %reshape.182) | data formatting | bytes 4194304 | tf_op jit(solution)/shard_map/reshape | solution.py:164
  2943.3 20.2 copy.92
  (59 shorter events, 7.0 us)
Async XLA Ops:
  7.2 234.6 %copy-start = (f32[20,4,32,128]{3,2,1,0:T(8,128)S(1)}, f32[20,4,32,128]{3,2,1,0:T(8,128)}, u32[]{:S(2)}) copy-start(f32[20,4,32,128]{3,2,1,0:T(8,128)} %param.17) | copy-start | bytes 3932164
  7.2 237.8 %all-gather.6.cloned.1.call-start = ((), (), s32[]{:S(2)}) async-start(), calls=%async_computation | async-start | bytes 8912896 | tf_op jit(solution)/shard_map/all_gather | solution.py:16
  8.0 26.8 copy-start.7
  38.0 557.6 %all-gather.8.cloned.1.call-start = ((), (), s32[]{:S(2)}) async-start(), calls=%async_computation.1 | async-start | bytes 44564480 | tf_op jit(solution)/shard_map/all_gather | solution.py:16
  48.7 2166.5 %all-gather.10.cloned.1.call-start = ((), (), s32[]{:S(2)}) async-start(), calls=%async_computation.2 | async-start | bytes 178257920 | tf_op jit(solution)/shard_map/all_gather | solution.py:16
  96.1 46.8 %copy-start.5 = (f32[20,20]{1,0:T(8,128)S(1)}, f32[20,20]{1,0:T(8,128)}, u32[]{:S(2)}) copy-start(f32[20,20]{1,0:T(8,128)} %param.15) | copy-start | bytes 4804
  96.1 46.9 %copy-start.4 = (f32[8,20,20]{2,0,1:T(8,128)S(1)}, f32[8,20,20]{2,0,1:T(8,128)}, u32[]{:S(2)}) copy-start(f32[8,20,20]{2,0,1:T(8,128)} %param.14) | copy-start | bytes 38404
  2447.9 98.9 %copy-start.2 = (f32[20,8,64,256]{3,0,2,1:T(8,128)}, f32[20,8,64,256]{3,0,2,1:T(8,128)S(1)}, u32[]{:S(2)}) copy-start(f32[20,8,64,256]{3,0,2,1:T(8,128)S(1)} %fusion.2) | copy-start | bytes 31457284
  2447.9 4.6 copy-start.8
  2448.7 423.0 %collective-permute-start.1 = (f32[20,8,1,256]{3,0,2,1:T(8,128)}, f32[20,8,1,256]{3,0,2,1:T(8,128)}, u32[]{:S(2)}, u32[]{:S(2)}) collective-permute-start(f32[20,8,1,256]{3,0,2,1:T(8,128)} %slice.47), channel_id=1, source_target_pairs={{1,0},{0,1},{3,2},{2,3},{5,4},{4,5},{7,6},{6,7},{9,8},{8,9},{11,10... | collective-permute-start | bytes 491528 | tf_op jit(solution)/shard_map/ppermute | solution.py:22
  2450.2 10.0 copy-start.12
  2450.2 444.1 %collective-permute-start = (f32[20,1,64,256]{3,2,1,0:T(8,128)}, f32[20,1,64,256]{3,2,1,0:T(8,128)}, u32[]{:S(2)}, u32[]{:S(2)}) collective-permute-start(f32[20,1,64,256]{3,2,1,0:T(8,128)} %copy.88), channel_id=1, source_target_pairs={{2,0},{4,2},{6,4},{8,6},{10,8},{12,10},{14,12},{16,14},{18,16},{20... | collective-permute-start | bytes 3932168 | tf_op jit(solution)/shard_map/ppermute | solution.py:22
  2460.3 86.5 %copy-start.6 = (f32[4,20,1,1]{1,0,3,2:T(4,128)S(1)}, f32[4,20,1,1]{1,0,3,2:T(4,128)}, u32[]{:S(2)}) copy-start(f32[4,20,1,1]{1,0,3,2:T(4,128)} %constant.108) | copy-start | bytes 964
  2688.0 183.6 %copy-start.11 = (f32[4,20,1]{1,0,2:T(4,128)S(1)}, f32[4,20,1]{1,0,2:T(4,128)}, u32[]{:S(2)}) copy-start(f32[4,20,1]{1,0,2:T(4,128)} %constant.112) | copy-start | bytes 964
  2688.0 184.8 %copy-start.3 = (f32[4,8,63,256]{3,0,2,1:T(4,128)S(1)}, f32[4,8,63,256]{3,0,2,1:T(4,128)}, u32[]{:S(2)}) copy-start(f32[4,8,63,256]{3,0,2,1:T(4,128)} %fusion.57) | copy-start | bytes 6193156
  2688.0 184.8 %copy-start.10 = (f32[4,20,1,1]{1,0,3,2:T(4,128)S(1)}, f32[4,20,1,1]{1,0,3,2:T(4,128)}, u32[]{:S(2)}) copy-start(f32[4,20,1,1]{1,0,3,2:T(4,128)} %constant.110) | copy-start | bytes 964
  2890.4 3.9 copy-start.13
  2890.4 6.9 copy-start.9
  2943.3 20.2 copy-start.1
Sparse Core Ops, SparseCore 0:
  38.1 116.1 all-gather.5
  157.0 438.5 all-gather.7
  598.4 1616.7 all-gather.9
